TPU v7x, 256 devices: a whole 4x4x8 slice. The times are simulated.
256 devices in a mesh: group: 8 (over y, core), dom: 32 (over z, x).
Axes of the slice: x: 4, y: 4, z: 8, core: 2. Of those that a mesh axis runs over, the one named last changes fastest.
Arguments:
- node_feats: bfloat16 [524288, 512], P(('group', 'dom')), may hold values from -36 to 36
- send_rows: int32 [256, 32, 32], P(('group', 'dom')), may hold values from 0 to 2047
- hub_rows: int32 [256, 8], P(('group', 'dom')), may hold values from 0 to 2047
- neighbours: int32 [524288, 16], P(('group', 'dom')), may hold values from 0 to 5119, as said below
- w_self: bfloat16 [512, 512], replicated, may hold values from -0.25 to 0.25
- w_neigh: bfloat16 [512, 512], replicated, may hold values from -0.25 to 0.25
- w_head: bfloat16 [512, 128], replicated, may hold values from -1.5 to 1.5
- s_first: bfloat16 [512, 512], replicated, may hold values from -0.25 to 0.25
- s_second: bfloat16 [512, 128], replicated, may hold values from -1.5 to 1.5
Outputs:
- teacher_hidden: bfloat16 [524288, 512], P(('group', 'dom'))
- grad_first: float32 [512, 512], replicated
- grad_second: float32 [512, 128], replicated
Inputs may be any that keep to these rules, and one draw needn't show every extreme that they name: `neighbours`: entries below 2048 are local rows; entries from 2048 to 3071 name halo rows, and from a given peer only its first rows, up to 32; the rest name hubs.
All inputs are finite; a program needn't handle non-finite values.
Results may differ from a plain program's by a relative error of at most 0.0025.
Values may be sent and summed in bfloat16 or wider, within the bound.
No kernel may reach another device: no remote copies, remote signals or barrier semaphores. Data moves between devices by JAX's collectives and lax.ppermute only.
A program may use at most 128 MiB of HBM per device.

v0:
```python
import jax
import jax.numpy as jnp
from jax import lax
from jax.sharding import PartitionSpec as P

DEG = 16
TEMPER = 2.0


def local_layer(feats, table, nbr, w_self, w_neigh, w_head, s_first, s_second, scale):
    rows = feats.shape[0]
    block = min(512, rows)

    def agg_block(index):
        picked = table[index].astype(jnp.float32)
        return (jnp.sum(picked, axis=1) / DEG).astype(jnp.bfloat16)

    agg = lax.map(agg_block, nbr.reshape(rows // block, block, DEG)).reshape(rows, feats.shape[1])
    pre = jnp.dot(feats, w_self, preferred_element_type=jnp.float32) + jnp.dot(
        agg, w_neigh, preferred_element_type=jnp.float32
    )
    hidden = jax.nn.relu(pre).astype(jnp.bfloat16)
    t_logits = jnp.dot(hidden, w_head, preferred_element_type=jnp.float32)
    s_pre = jnp.dot(feats, s_first, preferred_element_type=jnp.float32)
    s_hidden = jax.nn.relu(s_pre).astype(jnp.bfloat16)
    s_logits = jnp.dot(s_hidden, s_second, preferred_element_type=jnp.float32)
    p_teach = jax.nn.softmax(t_logits / TEMPER, axis=-1)
    p_stud = jax.nn.softmax(s_logits / TEMPER, axis=-1)
    delta = (TEMPER * (p_stud - p_teach) * scale).astype(jnp.bfloat16)
    g_second = jnp.dot(s_hidden.T, delta, preferred_element_type=jnp.float32)
    back = jnp.dot(delta, s_second.T, preferred_element_type=jnp.float32)
    back = jnp.where(s_pre > 0, back, 0.0).astype(jnp.bfloat16)
    g_first = jnp.dot(feats.T, back, preferred_element_type=jnp.float32)
    return (hidden, g_first, g_second)


def per_device(
    node_feats, send_rows, hub_rows, neighbours, w_self, w_neigh, w_head, s_first, s_second
):
    rows = node_feats.shape[0]
    width = node_feats.shape[1]
    outgoing = node_feats[send_rows[0]]
    received = lax.all_to_all(outgoing, "dom", split_axis=0, concat_axis=0, tiled=True)
    halo = received.reshape(-1, width)
    own_hubs = node_feats[hub_rows[0]]
    hubs = lax.all_gather(own_hubs, ("group", "dom"), axis=0, tiled=True)
    table = jnp.concatenate([node_feats, halo, hubs], axis=0)
    total_nodes = rows * lax.axis_size("group") * lax.axis_size("dom")
    scale = 1.0 / jnp.sqrt(jnp.float32(total_nodes))
    hidden, g_first, g_second = local_layer(
        node_feats, table, neighbours, w_self, w_neigh, w_head, s_first, s_second, scale
    )
    grad_first, grad_second = lax.psum((g_first, g_second), ("group", "dom"))
    return (hidden, grad_first, grad_second)


def solution(mesh):
    return jax.shard_map(
        per_device,
        mesh=mesh,
        in_specs=(
            P(("group", "dom"), None),
            P(("group", "dom"), None, None),
            P(("group", "dom"), None),
            P(("group", "dom"), None),
            P(),
            P(),
            P(),
            P(),
            P(),
        ),
        out_specs=(P(("group", "dom"), None), P(), P()),
        check_vma=False,
    )
```

profile of v0, /device:TPU:2, one launch (start us, length us, event | category | flops | bytes accessed | tf_op | source)
XLA Modules:
  0.0 601.0 jit_solution(7167910912744096948)
XLA Ops:
  7.9 3.0 gather_fusion.2
  11.8 7.1 %gather_fusion.1 = bf16[1024,512]{1,0:T(8,128)(2,1)} fusion(bf16[2048,512]{1,0:T(8,128)(2,1)} %param.11, s32[1024]{0:T(1024)S(1)} %broadcast_clamp_fusion.1), kind=kCustom, calls=%fused_computation.1 | custom fusion | bytes 2101248 | tf_op jit(solution)/shard_map/gather | solution.py:42
  18.9 11.7 %all-to-all-start = ((bf16[32,32,512]{2,1,0:T(8,128)(2,1)}), bf16[32,32,512]{2,1,0:T(8,128)(2,1)}, u32[]{:S(2)}, u32[]{:S(2)}) async-start(bf16[32,32,512]{2,1,0:T(8,128)(2,1)} %bitcast.43), calls=%async_computation | async-start | bytes 2097152 | tf_op jit(solution)/shard_map/all_to_all | solution.py:43
  33.2 1.9 copy-done.2
  35.1 1.8 fusion.12
  37.0 3.2 fusion.13
  40.2 18.6 %all-to-all-done = bf16[32,32,512]{2,1,0:T(8,128)(2,1)} async-done(((bf16[32,32,512]{2,1,0:T(8,128)(2,1)}), bf16[32,32,512]{2,1,0:T(8,128)(2,1)}, u32[]{:S(2)}, u32[]{:S(2)}) %all-to-all-start) | async-done | bytes 1048608 | tf_op jit(solution)/shard_map/all_to_all | solution.py:43
  58.8 61.9 %all-gather.3.cloned.1.call-done = bf16[2048,512]{1,0:T(8,128)(2,1)} async-done(((bf16[8,512]{1,0:T(8,128)(2,1)}), bf16[2048,512]{1,0:T(8,128)(2,1)}) %all-gather.3.cloned.1.call-update) | async-done | bytes 2097168 | tf_op jit(solution)/shard_map/all_gather | solution.py:46
  120.7 4.6 pad_maximum_fusion
  125.3 188.4 %while.10 = (s32[]{:T(128)}, bf16[4,512,512]{2,1,0:T(8,128)(2,1)}, s32[4,512,16]{2,1,0:T(8,128)}, bf16[5120,512]{1,0:T(8,128)(2,1)}, s32[]{:T(128)}) while((s32[]{:T(128)}, bf16[4,512,512]{2,1,0:T(8,128)(2,1)}, s32[4,512,16]{2,1,0:T(8,128)}, bf16[5120,512]{1,0:T(8,128)(2,1)}, s32[]{:T(128)}) %tuple.37), condition=%wide.region_2.3_spmd, body=%wide.region_0.2_spmd.sunk | while | flops 8683522 | bytes 28016716 | solution.py:18
  126.5 37.0 %gather_fusion = bf16[8192,512]{1,0:T(8,128)(2,1)} fusion(bf16[5120,512]{1,0:T(8,128)(2,1)} %get-tuple-element.90, s32[8192]{0:T(1024)S(1)} %broadcast_clamp_fusion.3), kind=kCustom, calls=%fused_computation.clone.1 | custom fusion | bytes 16809984 | tf_op jit(solution)/shard_map/while/body/eval_jaxpr/gather | solution.py:15
  163.5 8.0 %convert_reduce_fusion.2 = f32[512,512]{1,0:T(8,128)S(1)} fusion(bf16[8192,512]{1,0:T(8,128)(2,1)} %gather_fusion), kind=kLoop, calls=%fused_computation.3.clone.1 | loop fusion | flops 8126464 | bytes 9437184 | tf_op jit(solution)/shard_map/while/body/eval_jaxpr/reduce_sum | solution.py:16
  173.6 37.0 %gather_fusion = bf16[8192,512]{1,0:T(8,128)(2,1)} fusion(bf16[5120,512]{1,0:T(8,128)(2,1)} %get-tuple-element.90, s32[8192]{0:T(1024)S(1)} %broadcast_clamp_fusion.3), kind=kCustom, calls=%fused_computation.clone.1 | custom fusion | bytes 16809984 | tf_op jit(solution)/shard_map/while/body/eval_jaxpr/gather | solution.py:15
  210.6 8.0 %convert_reduce_fusion.2 = f32[512,512]{1,0:T(8,128)S(1)} fusion(bf16[8192,512]{1,0:T(8,128)(2,1)} %gather_fusion), kind=kLoop, calls=%fused_computation.3.clone.1 | loop fusion | flops 8126464 | bytes 9437184 | tf_op jit(solution)/shard_map/while/body/eval_jaxpr/reduce_sum | solution.py:16
  220.7 37.0 %gather_fusion = bf16[8192,512]{1,0:T(8,128)(2,1)} fusion(bf16[5120,512]{1,0:T(8,128)(2,1)} %get-tuple-element.90, s32[8192]{0:T(1024)S(1)} %broadcast_clamp_fusion.3), kind=kCustom, calls=%fused_computation.clone.1 | custom fusion | bytes 16809984 | tf_op jit(solution)/shard_map/while/body/eval_jaxpr/gather | solution.py:15
  257.7 8.0 %convert_reduce_fusion.2 = f32[512,512]{1,0:T(8,128)S(1)} fusion(bf16[8192,512]{1,0:T(8,128)(2,1)} %gather_fusion), kind=kLoop, calls=%fused_computation.3.clone.1 | loop fusion | flops 8126464 | bytes 9437184 | tf_op jit(solution)/shard_map/while/body/eval_jaxpr/reduce_sum | solution.py:16
  267.8 37.0 %gather_fusion = bf16[8192,512]{1,0:T(8,128)(2,1)} fusion(bf16[5120,512]{1,0:T(8,128)(2,1)} %get-tuple-element.90, s32[8192]{0:T(1024)S(1)} %broadcast_clamp_fusion.3), kind=kCustom, calls=%fused_computation.clone.1 | custom fusion | bytes 16809984 | tf_op jit(solution)/shard_map/while/body/eval_jaxpr/gather | solution.py:15
  304.8 8.0 %convert_reduce_fusion.2 = f32[512,512]{1,0:T(8,128)S(1)} fusion(bf16[8192,512]{1,0:T(8,128)(2,1)} %gather_fusion), kind=kLoop, calls=%fused_computation.3.clone.1 | loop fusion | flops 8126464 | bytes 9437184 | tf_op jit(solution)/shard_map/while/body/eval_jaxpr/reduce_sum | solution.py:16
  313.7 4.2 maximum_convert_fusion.1
  321.8 1.6 fusion.6
  323.4 6.0 %fusion.3 = f32[512,512]{0,1:T(8,128)} fusion(bf16[2048,512]{1,0:T(8,128)(2,1)S(1)} %copy-done.1, f32[2048,512]{1,0:T(8,128)} %copy-done.2, bf16[512,128]{1,0:T(8,128)(2,1)S(1)} %copy-done.12, f32[2048,128]{0,1:T(8,128)} %get-tuple-element.49, f32[2048,128]{0,1:T(8,128)} %copy-done.5, f32[2048]{0:T(1024)S(1)} %get-tuple-element.51, ...), kind=kOutput, calls=%fused_computation.16 | convolution fusion | flops 1347158016 | bytes 9601024 | tf_op jit(solution)/shard_map/dot_general | solution.py:33
  329.4 260.5 %all-reduce.3.cloned.1.call-done = (f32[512,512]{0,1:T(8,128)}, f32[512,128]{1,0:T(8,128)}) async-done(((f32[512,512]{0,1:T(8,128)}, f32[512,128]{1,0:T(8,128)}), (f32[512,512]{0,1:T(8,128)}, f32[512,128]{1,0:T(8,128)})) %all-reduce.3.cloned.1.call-update) | async-done | bytes 1310736 | tf_op jit(solution)/shard_map/psum | solution.py:53
  589.9 2.5 copy.14
  592.5 1.7 copy.27
  (55 shorter events, 16.3 us)
Async XLA Ops:
  7.2 24.8 %copy-start = (bf16[512,512]{1,0:T(8,128)(2,1)S(1)}, bf16[512,512]{1,0:T(8,128)(2,1)}, u32[]{:S(2)}) copy-start(bf16[512,512]{1,0:T(8,128)(2,1)} %param.18) | copy-start | bytes 1572868
  7.2 113.5 %all-gather.3.cloned.1.call-start = ((), (), s32[]{:S(2)}) async-start(), calls=%async_computation.1 | async-start | bytes 2105344 | tf_op jit(solution)/shard_map/all_gather | solution.py:46
  11.8 18.8 %copy-start.9 = (s32[2048,16]{0,1:T(8,128)S(1)}, s32[2048,16]{0,1:T(8,128)}, u32[]{:S(2)}) copy-start(s32[2048,16]{0,1:T(8,128)} %param.14) | copy-start | bytes 393220
  11.8 20.2 %copy-start.1 = (bf16[2048,512]{1,0:T(8,128)(2,1)S(1)}, bf16[2048,512]{1,0:T(8,128)(2,1)}, u32[]{:S(2)}) copy-start(bf16[2048,512]{1,0:T(8,128)(2,1)} %param.11) | copy-start | bytes 6291460
  18.9 39.9 %all-to-all-start = ((bf16[32,32,512]{2,1,0:T(8,128)(2,1)}), bf16[32,32,512]{2,1,0:T(8,128)(2,1)}, u32[]{:S(2)}, u32[]{:S(2)}) async-start(bf16[32,32,512]{2,1,0:T(8,128)(2,1)} %bitcast.43), calls=%async_computation | async-start | bytes 2097152 | tf_op jit(solution)/shard_map/all_to_all | solution.py:43
  30.6 559.4 %all-reduce.3.cloned.1.call-start = ((), (), s32[]{:S(2)}) async-start(), calls=%async_computation.2 | async-start | bytes 2621440 | tf_op jit(solution)/shard_map/psum | solution.py:53
  32.0 3.2 copy-start.11
  33.2 1.9 copy-start.2
  35.1 1.8 copy-start.7
  125.3 188.4 %copy-start.8 = (bf16[512,512]{1,0:T(8,128)(2,1)S(1)}, bf16[512,512]{1,0:T(8,128)(2,1)}, u32[]{:S(2)}) copy-start(bf16[512,512]{1,0:T(8,128)(2,1)} %param.16) | copy-start | bytes 1572868
  313.7 5.5 copy-start.10
  313.7 6.3 %copy-start.6 = (f32[2048,128]{0,1:T(8,128)S(1)}, f32[2048,128]{0,1:T(8,128)}, u32[]{:S(2)}) copy-start(f32[2048,128]{0,1:T(8,128)} %get-tuple-element.49) | copy-start | bytes 3145732
  317.9 1.3 copy-start.4
  319.2 2.6 copy-start.3
  320.1 1.0 copy-start.5
  321.8 1.6 copy-start.12
Sparse Core Ops, SparseCore 0:
  12.3 108.3 all-gather.2
  329.5 260.3 all-reduce.2
where the time goes:
time: 602 us; the launch traced here: 601 us
  waiting for transfers between devices  341 us (57%)
  local copies, waits for them, and re-layouts  169 us (28%)
  other arithmetic  46.2 us (8%)
  matrix products  18.9 us (3%)
  between operations  14.1 us (2%)
  starting transfers between devices  11.7 us (2%)
    psum x1, waiting for transfers between devices, per_device(): grad_first, grad_second = lax.psum((g_first, g_second), ('group', 'dom'))  261 us
    gather x4, local copies, waits for them, and re-layouts, agg_block(): picked = table[index].astype(jnp.float32)  148 us
    all_gather x1, waiting for transfers between devices, per_device(): hubs = lax.all_gather(own_hubs, ('group', 'dom'), axis=0, tiled=True)  61.9 us
    reduce_sum x4, other arithmetic, agg_block(): return (jnp.sum(picked, axis=1) / DEG).astype(jnp.bfloat16)  32.1 us
    all_to_all x1, waiting for transfers between devices, per_device(): lax.all_to_all(outgoing, 'dom', split_axis=0, concat_axis=0, tiled=True)  18.6 us
  transfers between devices with their start and end apart: 3, of which 3 were waited for; matrix products, arithmetic and copies ran while one was open for 3% of the time, Pallas kernels for 0%

commit v1 on v0

--- a/solution.py
+++ b/solution.py
@@ -50,7 +50,7 @@
     hidden, g_first, g_second = local_layer(
         node_feats, table, neighbours, w_self, w_neigh, w_head, s_first, s_second, scale
     )
-    grad_first, grad_second = lax.psum((g_first, g_second), ("group", "dom"))
+    grad_first, grad_second = lax.psum(lax.psum((g_first, g_second), "group"), "dom")
     return (hidden, grad_first, grad_second)
 
 

time: 602 us -> 563 us (0.935)
  waiting for transfers between devices: 341 us -> 301 us
    psum x1 -> x2, waiting for transfers between devices: 261 us -> 221 us  [the longest x1 153 us: per_device(): lax.psum(lax.psum((g_first, g_second), 'group'), 'dom')]
  transfers between devices with their start and end apart: 3 -> 4, of which waited for: 3 -> 4; matrix products, arithmetic and copies ran while one was open for 3% -> 3% of each run, Pallas kernels for 0% -> 0%
where the time goes in v1:
time: 563 us; the launch traced here: 561 us
  waiting for transfers between devices  301 us (53%)
  local copies, waits for them, and re-layouts  169 us (30%)
  other arithmetic  46.2 us (8%)
  matrix products  18.9 us (3%)
  between operations  13.8 us (2%)
  starting transfers between devices  11.8 us (2%)
    psum x1, waiting for transfers between devices, per_device(): lax.psum(lax.psum((g_first, g_second), 'group'), 'dom')  153 us
    gather x4, local copies, waits for them, and re-layouts, agg_block(): picked = table[index].astype(jnp.float32)  148 us
    psum x1, waiting for transfers between devices, per_device(): lax.psum((g_first, g_second), 'group')  67.7 us
    all_gather x1, waiting for transfers between devices, per_device(): hubs = lax.all_gather(own_hubs, ('group', 'dom'), axis=0, tiled=True)  61.9 us
    reduce_sum x4, other arithmetic, agg_block(): return (jnp.sum(picked, axis=1) / DEG).astype(jnp.bfloat16)  32.1 us
    all_to_all x1, waiting for transfers between devices, per_device(): lax.all_to_all(outgoing, 'dom', split_axis=0, concat_axis=0, tiled=True)  18.6 us
    all_to_all x1, starting transfers between devices, per_device(): lax.all_to_all(outgoing, 'dom', split_axis=0, concat_axis=0, tiled=True)  11.7 us
  transfers between devices with their start and end apart: 4, of which 4 were waited for; matrix products, arithmetic and copies ran while one was open for 3% of the time, Pallas kernels for 0%

profile of v1, /device:TPU:2, one launch (start us, length us, event | category | flops | bytes accessed | tf_op | source)
XLA Modules:
  0.0 561.0 jit_solution(6870264504949153211)
XLA Ops:
  7.9 3.0 gather_fusion.2
  11.8 7.1 %gather_fusion.1 = bf16[1024,512]{1,0:T(8,128)(2,1)} fusion(bf16[2048,512]{1,0:T(8,128)(2,1)} %param.11, s32[1024]{0:T(1024)S(1)} %broadcast_clamp_fusion.1), kind=kCustom, calls=%fused_computation.1 | custom fusion | bytes 2101248 | tf_op jit(solution)/shard_map/gather | solution.py:42
  18.9 11.7 %all-to-all-start = ((bf16[32,32,512]{2,1,0:T(8,128)(2,1)}), bf16[32,32,512]{2,1,0:T(8,128)(2,1)}, u32[]{:S(2)}, u32[]{:S(2)}) async-start(bf16[32,32,512]{2,1,0:T(8,128)(2,1)} %bitcast.43), calls=%async_computation | async-start | bytes 2097152 | tf_op jit(solution)/shard_map/all_to_all | solution.py:43
  33.2 1.9 copy-done.2
  35.2 1.8 fusion.12
  37.0 3.2 fusion.13
  40.2 18.6 %all-to-all-done = bf16[32,32,512]{2,1,0:T(8,128)(2,1)} async-done(((bf16[32,32,512]{2,1,0:T(8,128)(2,1)}), bf16[32,32,512]{2,1,0:T(8,128)(2,1)}, u32[]{:S(2)}, u32[]{:S(2)}) %all-to-all-start) | async-done | bytes 1048608 | tf_op jit(solution)/shard_map/all_to_all | solution.py:43
  58.8 61.9 %all-gather.3.cloned.1.call-done = bf16[2048,512]{1,0:T(8,128)(2,1)} async-done(((bf16[8,512]{1,0:T(8,128)(2,1)}), bf16[2048,512]{1,0:T(8,128)(2,1)}) %all-gather.3.cloned.1.call-update) | async-done | bytes 2097168 | tf_op jit(solution)/shard_map/all_gather | solution.py:46
  120.7 4.6 pad_maximum_fusion
  125.3 188.2 %while.10 = (s32[]{:T(128)}, bf16[4,512,512]{2,1,0:T(8,128)(2,1)}, s32[4,512,16]{2,1,0:T(8,128)}, bf16[5120,512]{1,0:T(8,128)(2,1)}, s32[]{:T(128)}) while((s32[]{:T(128)}, bf16[4,512,512]{2,1,0:T(8,128)(2,1)}, s32[4,512,16]{2,1,0:T(8,128)}, bf16[5120,512]{1,0:T(8,128)(2,1)}, s32[]{:T(128)}) %tuple.40), condition=%wide.region_2.3_spmd, body=%wide.region_0.2_spmd.sunk | while | flops 8683522 | bytes 28016716 | solution.py:18
  126.5 37.0 %gather_fusion = bf16[8192,512]{1,0:T(8,128)(2,1)} fusion(bf16[5120,512]{1,0:T(8,128)(2,1)} %get-tuple-element.92, s32[8192]{0:T(1024)S(1)} %broadcast_clamp_fusion.3), kind=kCustom, calls=%fused_computation.clone.1 | custom fusion | bytes 16809984 | tf_op jit(solution)/shard_map/while/body/eval_jaxpr/gather | solution.py:15
  163.5 8.0 %convert_reduce_fusion.2 = f32[512,512]{1,0:T(8,128)S(1)} fusion(bf16[8192,512]{1,0:T(8,128)(2,1)} %gather_fusion), kind=kLoop, calls=%fused_computation.3.clone.1 | loop fusion | flops 8126464 | bytes 9437184 | tf_op jit(solution)/shard_map/while/body/eval_jaxpr/reduce_sum | solution.py:16
  173.6 37.0 %gather_fusion = bf16[8192,512]{1,0:T(8,128)(2,1)} fusion(bf16[5120,512]{1,0:T(8,128)(2,1)} %get-tuple-element.92, s32[8192]{0:T(1024)S(1)} %broadcast_clamp_fusion.3), kind=kCustom, calls=%fused_computation.clone.1 | custom fusion | bytes 16809984 | tf_op jit(solution)/shard_map/while/body/eval_jaxpr/gather | solution.py:15
  210.5 8.0 %convert_reduce_fusion.2 = f32[512,512]{1,0:T(8,128)S(1)} fusion(bf16[8192,512]{1,0:T(8,128)(2,1)} %gather_fusion), kind=kLoop, calls=%fused_computation.3.clone.1 | loop fusion | flops 8126464 | bytes 9437184 | tf_op jit(solution)/shard_map/while/body/eval_jaxpr/reduce_sum | solution.py:16
  220.6 37.0 %gather_fusion = bf16[8192,512]{1,0:T(8,128)(2,1)} fusion(bf16[5120,512]{1,0:T(8,128)(2,1)} %get-tuple-element.92, s32[8192]{0:T(1024)S(1)} %broadcast_clamp_fusion.3), kind=kCustom, calls=%fused_computation.clone.1 | custom fusion | bytes 16809984 | tf_op jit(solution)/shard_map/while/body/eval_jaxpr/gather | solution.py:15
  257.6 8.0 %convert_reduce_fusion.2 = f32[512,512]{1,0:T(8,128)S(1)} fusion(bf16[8192,512]{1,0:T(8,128)(2,1)} %gather_fusion), kind=kLoop, calls=%fused_computation.3.clone.1 | loop fusion | flops 8126464 | bytes 9437184 | tf_op jit(solution)/shard_map/while/body/eval_jaxpr/reduce_sum | solution.py:16
  267.7 37.0 %gather_fusion = bf16[8192,512]{1,0:T(8,128)(2,1)} fusion(bf16[5120,512]{1,0:T(8,128)(2,1)} %get-tuple-element.92, s32[8192]{0:T(1024)S(1)} %broadcast_clamp_fusion.3), kind=kCustom, calls=%fused_computation.clone.1 | custom fusion | bytes 16809984 | tf_op jit(solution)/shard_map/while/body/eval_jaxpr/gather | solution.py:15
  304.6 8.0 %convert_reduce_fusion.2 = f32[512,512]{1,0:T(8,128)S(1)} fusion(bf16[8192,512]{1,0:T(8,128)(2,1)} %gather_fusion), kind=kLoop, calls=%fused_computation.3.clone.1 | loop fusion | flops 8126464 | bytes 9437184 | tf_op jit(solution)/shard_map/while/body/eval_jaxpr/reduce_sum | solution.py:16
  313.6 4.2 maximum_convert_fusion.1
  323.2 6.0 %fusion.3 = f32[512,512]{0,1:T(8,128)} fusion(bf16[2048,512]{1,0:T(8,128)(2,1)S(1)} %copy-done.1, f32[2048,512]{1,0:T(8,128)} %copy-done.2, bf16[512,128]{1,0:T(8,128)(2,1)S(1)} %copy-done.12, f32[2048,128]{0,1:T(8,128)} %get-tuple-element.51, f32[2048,128]{0,1:T(8,128)} %copy-done.5, f32[2048]{0:T(1024)S(1)} %get-tuple-element.53, ...), kind=kOutput, calls=%fused_computation.16 | convolution fusion | flops 1347158016 | bytes 9601024 | tf_op jit(solution)/shard_map/dot_general | solution.py:33
  329.3 67.7 %all-reduce.7.cloned.1.call-done = (f32[512,512]{0,1:T(8,128)}, f32[512,128]{1,0:T(8,128)}) async-done(((f32[512,512]{0,1:T(8,128)}, f32[512,128]{1,0:T(8,128)}), (f32[512,512]{0,1:T(8,128)}, f32[512,128]{1,0:T(8,128)})) %all-reduce.7.cloned.1.call-update) | async-done | bytes 1310736 | tf_op jit(solution)/shard_map/psum | solution.py:53
  397.0 153.2 %all-reduce.5.cloned.1.call-done = (f32[512,512]{0,1:T(8,128)}, f32[512,128]{1,0:T(8,128)}) async-done(((f32[512,512]{0,1:T(8,128)}, f32[512,128]{1,0:T(8,128)}), (f32[512,512]{0,1:T(8,128)}, f32[512,128]{1,0:T(8,128)})) %all-reduce.5.cloned.1.call-update) | async-done | bytes 1310736 | tf_op jit(solution)/shard_map/psum | solution.py:53
  550.2 2.5 copy.14
  552.8 1.7 copy.29
  (58 shorter events, 17.9 us)
Async XLA Ops:
  7.2 24.8 %copy-start = (bf16[512,512]{1,0:T(8,128)(2,1)S(1)}, bf16[512,512]{1,0:T(8,128)(2,1)}, u32[]{:S(2)}) copy-start(bf16[512,512]{1,0:T(8,128)(2,1)} %param.18) | copy-start | bytes 1572868
  7.2 113.6 %all-gather.3.cloned.1.call-start = ((), (), s32[]{:S(2)}) async-start(), calls=%async_computation.1 | async-start | bytes 2105344 | tf_op jit(solution)/shard_map/all_gather | solution.py:46
  11.8 18.9 %copy-start.9 = (s32[2048,16]{0,1:T(8,128)S(1)}, s32[2048,16]{0,1:T(8,128)}, u32[]{:S(2)}) copy-start(s32[2048,16]{0,1:T(8,128)} %param.14) | copy-start | bytes 393220
  11.8 20.2 %copy-start.1 = (bf16[2048,512]{1,0:T(8,128)(2,1)S(1)}, bf16[2048,512]{1,0:T(8,128)(2,1)}, u32[]{:S(2)}) copy-start(bf16[2048,512]{1,0:T(8,128)(2,1)} %param.11) | copy-start | bytes 6291460
  18.9 39.9 %all-to-all-start = ((bf16[32,32,512]{2,1,0:T(8,128)(2,1)}), bf16[32,32,512]{2,1,0:T(8,128)(2,1)}, u32[]{:S(2)}, u32[]{:S(2)}) async-start(bf16[32,32,512]{2,1,0:T(8,128)(2,1)} %bitcast.43), calls=%async_computation | async-start | bytes 2097152 | tf_op jit(solution)/shard_map/all_to_all | solution.py:43
  30.6 366.4 %all-reduce.7.cloned.1.call-start = ((), (), s32[]{:S(2)}) async-start(), calls=%async_computation.3 | async-start | bytes 2621440 | tf_op jit(solution)/shard_map/psum | solution.py:53
  32.0 3.2 copy-start.11
  33.2 1.9 copy-start.2
  35.2 1.8 copy-start.7
  125.3 188.2 %copy-start.8 = (bf16[512,512]{1,0:T(8,128)(2,1)S(1)}, bf16[512,512]{1,0:T(8,128)(2,1)}, u32[]{:S(2)}) copy-start(bf16[512,512]{1,0:T(8,128)(2,1)} %param.16) | copy-start | bytes 1572868
  313.6 5.5 copy-start.10
  313.6 6.3 %copy-start.6 = (f32[2048,128]{0,1:T(8,128)S(1)}, f32[2048,128]{0,1:T(8,128)}, u32[]{:S(2)}) copy-start(f32[2048,128]{0,1:T(8,128)} %get-tuple-element.51) | copy-start | bytes 3145732
  317.8 1.3 copy-start.4
  319.1 2.6 copy-start.3
  319.9 1.0 copy-start.5
  321.6 1.6 copy-start.12
  329.3 221.0 %all-reduce.5.cloned.1.call-start = ((), (), s32[]{:S(2)}) async-start(), calls=%async_computation.2 | async-start | bytes 2621440 | tf_op jit(solution)/shard_map/psum | solution.py:53
Sparse Core Ops, SparseCore 0:
  12.3 108.4 all-gather.2
  329.4 67.5 all-reduce.6
  400.5 149.6 all-reduce.4
